TPU v7x, 128 devices: a whole 4x4x4 slice. The times are simulated.
128 devices in a mesh: section: 2 (over core), blk: 16 (over y, x), mp: 4 (over z).
Axes of the slice: x: 4, y: 4, z: 4, core: 2. Of those that a mesh axis runs over, the one named last changes fastest.
Arguments:
- patches: bfloat16 [256, 5120], P('section'), may hold values from -6 to 6
- merge_gain: float32 [1280], replicated, may hold values from 0.25 to 1.75
- merge_first: bfloat16 [5120, 5120], P(None, ('blk', 'mp')), may hold values from -0.078125 to 0.078125
- merge_second: bfloat16 [5120, 4096], P(('blk', 'mp')), may hold values from -0.078125 to 0.078125
- text_embeds: bfloat16 [4, 1024, 4096], P(None, 'blk', 'mp'), may hold values from -7 to 14
- positions: int32 [256], replicated, may hold values from 0 to 4095, as said below
- segments: int32 [4096], replicated, may hold values from 0 to 2, never falling along the last dimension, each value on 1 to 2048 neighbouring positions
- norm_gain: float32 [2, 4096], P('section'), may hold values from 0.25 to 1.75
- query_weight: bfloat16 [2, 4096, 4096], P('section', 'blk', 'mp'), may hold values from -1 to 1
- keyval_weight: bfloat16 [2, 4096, 4, 2, 128], P('section', 'blk', 'mp'), may hold values from -1 to 1
- out_weight: bfloat16 [2, 4096, 4096], P('section', 'mp', 'blk'), may hold values from -0.09375 to 0.09375
Outputs:
- hidden: bfloat16 [2, 4, 1024, 4096], P('section', None, 'blk', 'mp')
Inputs may be any that keep to these rules, and one draw needn't show every extreme that they name: `positions`: distinct and increasing.
All inputs are finite; a program needn't handle non-finite values.
Results may differ from a plain program's by a relative error of at most 0.015.
Values may be sent and summed in bfloat16 or wider, within the bound.
No kernel may reach another device: no remote copies, remote signals or barrier semaphores. Data moves between devices by JAX's collectives and lax.ppermute only.
A program may use at most 128 MiB of HBM per device.

v0:
```python
import jax
import jax.numpy as jnp
from jax import lax
from jax.sharding import PartitionSpec as P

epsilon = 1e-06
rope_base = 1000000.0


def shifted(value, axis, by):
    size = lax.axis_size(axis)
    pairs = [(i, i + by) for i in range(size) if 0 <= i + by < size]
    return lax.ppermute(value, axis, pairs)


def rope_tables(where_at, head_size):
    steps_half = jnp.arange(head_size // 2).astype(jnp.float32)
    inverse = jnp.exp(-jnp.log(rope_base) * 2.0 * steps_half / head_size)
    angles = where_at.astype(jnp.float32)[:, None] * inverse[None, :]
    return (jnp.cos(angles), jnp.sin(angles))


def rotate(values, cosine, sine):
    half = values.shape[-1] // 2
    first = values[..., :half]
    second = values[..., half:]
    cosine = cosine[:, None, :]
    sine = sine[:, None, :]
    return jnp.concatenate(
        [first * cosine - second * sine, second * cosine + first * sine], axis=-1
    )


def local(
    patches,
    merge_gain,
    merge_first,
    merge_second,
    text_embeds,
    positions,
    segments,
    norm_gain,
    query_weight,
    keyval_weight,
    out_weight,
):
    count = patches.shape[0]
    width = merge_gain.shape[0]
    blocks = text_embeds.shape[0]
    rows_here = text_embeds.shape[1]
    slice_width = text_embeds.shape[2]
    seq_len = segments.shape[0]
    block_len = seq_len // blocks
    section_index = lax.axis_index("section")
    cycle_index = lax.axis_index("blk")
    model_index = lax.axis_index("mp")
    pieces = patches.astype(jnp.float32).reshape(count, -1, width)
    centered = pieces - jnp.mean(pieces, axis=-1, keepdims=True)
    variance = jnp.mean(centered * centered, axis=-1, keepdims=True)
    normed = (
        (centered * lax.rsqrt(variance + epsilon) * merge_gain)
        .reshape(count, -1)
        .astype(jnp.bfloat16)
    )
    inner = jax.nn.gelu(
        jnp.dot(normed, merge_first, preferred_element_type=jnp.float32), approximate=False
    ).astype(jnp.bfloat16)
    partial_merge = jnp.dot(inner, merge_second, preferred_element_type=jnp.float32)
    merged_full = lax.psum(partial_merge, ("blk", "mp")).astype(jnp.bfloat16)
    merged_mine = lax.dynamic_slice_in_dim(merged_full, model_index * slice_width, slice_width, 1)
    visual_all = lax.all_gather(merged_mine, "section", axis=0, tiled=True)
    query_full, keyval_full, out_full = (
        lax.all_gather(query_weight, "blk", axis=1, tiled=True),
        lax.all_gather(keyval_weight, "blk", axis=1, tiled=True),
        lax.all_gather(out_weight, "blk", axis=2, tiled=True),
    )
    query_full = query_full[0]
    kv_heads = keyval_full.shape[2]
    head_size = keyval_full.shape[4]
    keyval_full = keyval_full[0].reshape(keyval_full.shape[1], -1)
    out_full = out_full[0]
    gain_here = norm_gain[0]
    group = query_full.shape[1] // (kv_heads * head_size)
    scale = 1.0 / head_size**0.5
    key_where = jnp.arange(seq_len)
    ticks = blocks + lax.axis_size("section") - 1
    zero_index = jnp.zeros((), jnp.int32)
    held = jnp.zeros((rows_here, slice_width), jnp.bfloat16)
    cache_keys = jnp.zeros((seq_len, kv_heads, head_size), jnp.bfloat16)
    cache_values = jnp.zeros((seq_len, kv_heads, head_size), jnp.bfloat16)
    outputs = jnp.zeros((blocks, rows_here, slice_width), jnp.bfloat16)
    for tick_now in range(ticks):
        bound = min(tick_now + 1, blocks) * block_len
        block_now = tick_now - section_index
        active = (block_now >= 0) & (block_now < blocks)
        block_safe = jnp.clip(block_now, 0, blocks - 1)
        row_where = block_safe * block_len + cycle_index * rows_here + jnp.arange(rows_here)
        is_visual = positions[None, :] == row_where[:, None]
        picked = jnp.dot(
            is_visual.astype(jnp.bfloat16), visual_all, preferred_element_type=jnp.float32
        ).astype(jnp.bfloat16)
        text_rows = lax.dynamic_index_in_dim(text_embeds, block_safe, 0, keepdims=False)
        embedded = jnp.where(jnp.any(is_visual, axis=1)[:, None], picked, text_rows)
        incoming = jnp.where(section_index == 0, embedded, held)
        features = lax.all_gather(incoming, "mp", axis=1, tiled=True)
        feat_f = features.astype(jnp.float32)
        normx = (
            feat_f
            * lax.rsqrt(jnp.mean(feat_f * feat_f, axis=-1, keepdims=True) + epsilon)
            * gain_here
        ).astype(jnp.bfloat16)
        cosine, sine = rope_tables(row_where, head_size)
        query = jnp.dot(normx, query_full, preferred_element_type=jnp.float32).reshape(
            rows_here, -1, head_size
        )
        query = (
            rotate(query, cosine, sine)
            .astype(jnp.bfloat16)
            .reshape(rows_here, kv_heads, group, head_size)
        )
        keyval = jnp.dot(normx, keyval_full, preferred_element_type=jnp.float32).reshape(
            rows_here, kv_heads, 2, head_size
        )
        new_keys = rotate(keyval[:, :, 0, :], cosine, sine).astype(jnp.bfloat16)
        new_values = keyval[:, :, 1, :].astype(jnp.bfloat16)
        block_keys, block_values = (
            lax.all_gather(new_keys, "blk", axis=0, tiled=True),
            lax.all_gather(new_values, "blk", axis=0, tiled=True),
        )
        start = block_safe * block_len
        cache_keys = jnp.where(
            active,
            lax.dynamic_update_slice(cache_keys, block_keys, (start, zero_index, zero_index)),
            cache_keys,
        )
        cache_values = jnp.where(
            active,
            lax.dynamic_update_slice(cache_values, block_values, (start, zero_index, zero_index)),
            cache_values,
        )
        keys_seen = cache_keys[:bound]
        values_seen = cache_values[:bound]
        scores = (
            jnp.einsum("qkgd,skd->kgqs", query, keys_seen, preferred_element_type=jnp.float32)
            * scale
        )
        row_segments = jnp.take(segments, row_where)
        allowed = (key_where[None, :bound] <= row_where[:, None]) & (
            segments[None, :bound] == row_segments[:, None]
        )
        scores = jnp.where(allowed[None, None], scores, -jnp.inf)
        top = jnp.max(scores, axis=-1, keepdims=True)
        expo = jnp.exp(scores - top)
        probs = (expo / jnp.sum(expo, axis=-1, keepdims=True)).astype(jnp.bfloat16)
        attended = jnp.einsum(
            "kgqs,skd->qkgd", probs, values_seen, preferred_element_type=jnp.float32
        )
        attended = attended.reshape(rows_here, -1).astype(jnp.bfloat16)
        term = jnp.dot(attended, out_full, preferred_element_type=jnp.float32)
        summed = lax.psum_scatter(
            term.astype(jnp.bfloat16), "mp", scatter_dimension=1, tiled=True
        ).astype(jnp.float32)
        result = (incoming.astype(jnp.float32) + summed).astype(jnp.bfloat16)
        outputs = jnp.where(
            active,
            lax.dynamic_update_slice(outputs, result[None], (block_safe, zero_index, zero_index)),
            outputs,
        )
        held = shifted(result, "section", 1)
    return outputs[None]


def solution(mesh):
    return jax.shard_map(
        local,
        mesh=mesh,
        in_specs=(
            P("section", None),
            P(),
            P(None, ("blk", "mp")),
            P(("blk", "mp"), None),
            P(None, "blk", "mp"),
            P(),
            P(),
            P("section", None),
            P("section", "blk", "mp"),
            P("section", "blk", "mp", None, None),
            P("section", "mp", "blk"),
        ),
        out_specs=P("section", None, "blk", "mp"),
        check_vma=False,
    )
```

profile of v0, /device:TPU:0, one launch (start us, length us, event | category | flops | bytes accessed | tf_op | source)
XLA Modules:
  0.0 948.9 jit_solution(6913599249277682439)
XLA Ops:
  8.8 2.9 reshape.1266
  14.3 1.9 copy.38
  16.2 5.2 fusion.210
  23.5 383.3 %all-reduce.1 = bf16[128,4096]{1,0:T(8,128)(2,1)S(1)} all-reduce(f32[128,4096]{1,0:T(8,128)} %fusion.210), channel_id=1, replica_groups=mesh['section'=2,'blk'=16,'mp'=4] {'blk','mp'}, use_global_device_ids=true, to_apply=%region_3.4 | all-reduce | flops 524288 | bytes 3145728 | tf_op jit(solution)/shard_map/psum | solution.py:69
  407.7 2.2 all_gather.57
  411.0 13.4 %all_gather.58 = bf16[64,4096]{1,0:T(8,128)(2,1)S(1)} all-gather(bf16[64,1024]{1,0:T(8,128)(2,1)S(1)} %fusion.63), channel_id=1, replica_groups=mesh['section'=2,'blk'=16,'mp'=4] {'mp'}, dimensions={1}, use_global_device_ids=true | all-gather | bytes 655360 | tf_op jit(solution)/shard_map/all_gather | solution.py:105
  426.1 4.7 copy.37
  432.0 20.7 %all_gather.61 = bf16[1024,1,128]{2,0,1:T(8,128)(2,1)S(1)} all-gather(bf16[64,1,128]{2,0,1:T(8,128)(2,1)S(1)} %pad_maximum_fusion), channel_id=1, replica_groups=mesh['section'=2,'blk'=16,'mp'=4] {'blk'}, dimensions={0}, use_global_device_ids=true | all-gather | bytes 278528 | tf_op jit(solution)/shard_map/all_gather | solution.py:127
  452.7 24.1 %all-gather = bf16[1024,1,1,128]{3,0,2,1:T(8,128)(2,1)S(1)} all-gather(bf16[64,1,1,128]{3,0,2,1:T(8,128)(2,1)S(1)} %slice.285), channel_id=2, replica_groups=mesh['section'=2,'blk'=16,'mp'=4] {'blk'}, dimensions={0}, use_global_device_ids=true | all-gather | bytes 278528 | tf_op jit(solution)/shard_map/all_gather | solution.py:128
  480.5 11.8 %copy.31 = bf16[1024,4096]{1,0:T(8,128)(2,1)} copy(bf16[1024,4096]{0,1:T(8,128)(2,1)} %bitcast.333) | data formatting | bytes 16777216 | tf_op jit(solution)/shard_map/dot_general | solution.py:113
  492.3 6.1 fusion.125
  502.2 5.8 fusion.13
  511.2 15.4 %reduce-scatter.6.cloned.1.call-done = bf16[64,1024]{1,0:T(8,128)(2,1)} async-done(((bf16[64,4096]{1,0:T(8,128)(2,1)}), bf16[64,1024]{1,0:T(8,128)(2,1)}) %reduce-scatter.6.cloned.1.call-update) | async-done | bytes 131088 | tf_op jit(solution)/shard_map/reduce_scatter | solution.py:160
  531.9 13.5 %all_gather.64 = bf16[64,4096]{1,0:T(8,128)(2,1)S(1)} all-gather(bf16[64,1024]{1,0:T(8,128)(2,1)S(1)} %fusion.65), channel_id=1, replica_groups=mesh['section'=2,'blk'=16,'mp'=4] {'mp'}, dimensions={1}, use_global_device_ids=true | all-gather | bytes 655360 | tf_op jit(solution)/shard_map/all_gather | solution.py:105
  546.5 6.1 fusion.128
  552.6 23.8 %all-gather.1 = bf16[1024,1,1,128]{3,0,2,1:T(8,128)(2,1)S(1)} all-gather(bf16[64,1,1,128]{3,0,2,1:T(8,128)(2,1)S(1)} %slice.284), channel_id=3, replica_groups=mesh['section'=2,'blk'=16,'mp'=4] {'blk'}, dimensions={0}, use_global_device_ids=true | all-gather | bytes 278528 | tf_op jit(solution)/shard_map/all_gather | solution.py:128
  576.7 23.3 %all_gather.66 = bf16[1024,1,128]{2,0,1:T(8,128)(2,1)S(1)} all-gather(bf16[64,1,128]{2,0,1:T(8,128)(2,1)S(1)} %pad_maximum_fusion.1), channel_id=1, replica_groups=mesh['section'=2,'blk'=16,'mp'=4] {'blk'}, dimensions={0}, use_global_device_ids=true | all-gather | bytes 278528 | tf_op jit(solution)/shard_map/all_gather | solution.py:127
  599.9 1.7 fusion.142
  603.6 2.0 fusion.312
  606.2 2.2 fusion.69
  609.4 2.4 fusion.16
  616.2 14.5 %reduce-scatter.8.cloned.1.call-done = bf16[64,1024]{1,0:T(8,128)(2,1)} async-done(((bf16[64,4096]{1,0:T(8,128)(2,1)}), bf16[64,1024]{1,0:T(8,128)(2,1)}) %reduce-scatter.8.cloned.1.call-update) | async-done | bytes 131088 | tf_op jit(solution)/shard_map/reduce_scatter | solution.py:160
  633.9 13.5 %all_gather.67 = bf16[64,4096]{1,0:T(8,128)(2,1)S(1)} all-gather(bf16[64,1024]{1,0:T(8,128)(2,1)S(1)} %broadcast_select_fusion.2), channel_id=1, replica_groups=mesh['section'=2,'blk'=16,'mp'=4] {'mp'}, dimensions={1}, use_global_device_ids=true | all-gather | bytes 655360 | tf_op jit(solution)/shard_map/all_gather | solution.py:105
  648.5 6.1 fusion.131
  654.6 23.8 %all-gather.2 = bf16[1024,1,1,128]{3,0,2,1:T(8,128)(2,1)S(1)} all-gather(bf16[64,1,1,128]{3,0,2,1:T(8,128)(2,1)S(1)} %slice.283), channel_id=4, replica_groups=mesh['section'=2,'blk'=16,'mp'=4] {'blk'}, dimensions={0}, use_global_device_ids=true | all-gather | bytes 278528 | tf_op jit(solution)/shard_map/all_gather | solution.py:128
  678.7 23.4 %all_gather.69 = bf16[1024,1,128]{2,0,1:T(8,128)(2,1)S(1)} all-gather(bf16[64,1,128]{2,0,1:T(8,128)(2,1)S(1)} %pad_maximum_fusion.2), channel_id=1, replica_groups=mesh['section'=2,'blk'=16,'mp'=4] {'blk'}, dimensions={0}, use_global_device_ids=true | all-gather | bytes 278528 | tf_op jit(solution)/shard_map/all_gather | solution.py:127
  702.1 1.7 fusion.141
  703.8 1.7 select_dynamic-update-slice_fusion.1
  705.7 2.4 fusion.313
  709.1 2.5 fusion.79
  712.1 2.4 fusion.19
  715.8 17.7 %reduce-scatter.10.cloned.1.call-done = bf16[64,1024]{1,0:T(8,128)(2,1)} async-done(((bf16[64,4096]{1,0:T(8,128)(2,1)}), bf16[64,1024]{1,0:T(8,128)(2,1)}) %reduce-scatter.10.cloned.1.call-update) | async-done | bytes 131088 | tf_op jit(solution)/shard_map/reduce_scatter | solution.py:160
  737.7 13.4 %all_gather.70 = bf16[64,4096]{1,0:T(8,128)(2,1)S(1)} all-gather(bf16[64,1024]{1,0:T(8,128)(2,1)S(1)} %broadcast_select_fusion.1), channel_id=1, replica_groups=mesh['section'=2,'blk'=16,'mp'=4] {'mp'}, dimensions={1}, use_global_device_ids=true | all-gather | bytes 655360 | tf_op jit(solution)/shard_map/all_gather | solution.py:105
  752.1 6.1 fusion.134
  758.2 23.8 %all-gather.3 = bf16[1024,1,1,128]{3,0,2,1:T(8,128)(2,1)S(1)} all-gather(bf16[64,1,1,128]{3,0,2,1:T(8,128)(2,1)S(1)} %slice.282), channel_id=5, replica_groups=mesh['section'=2,'blk'=16,'mp'=4] {'blk'}, dimensions={0}, use_global_device_ids=true | all-gather | bytes 278528 | tf_op jit(solution)/shard_map/all_gather | solution.py:128
  782.3 23.2 %all_gather.72 = bf16[1024,1,128]{2,0,1:T(8,128)(2,1)S(1)} all-gather(bf16[64,1,128]{2,0,1:T(8,128)(2,1)S(1)} %pad_maximum_fusion.3), channel_id=1, replica_groups=mesh['section'=2,'blk'=16,'mp'=4] {'blk'}, dimensions={0}, use_global_device_ids=true | all-gather | bytes 278528 | tf_op jit(solution)/shard_map/all_gather | solution.py:127
  805.5 1.7 fusion.140
  807.2 1.7 select_dynamic-update-slice_fusion
  809.1 2.9 fusion.314
  813.3 2.8 fusion.76
  816.2 2.4 fusion.22
  818.7 18.8 %reduce-scatter.12.cloned.1.call-done = bf16[64,1024]{1,0:T(8,128)(2,1)} async-done(((bf16[64,4096]{1,0:T(8,128)(2,1)}), bf16[64,1024]{1,0:T(8,128)(2,1)}) %reduce-scatter.12.cloned.1.call-update) | async-done | bytes 131088 | tf_op jit(solution)/shard_map/reduce_scatter | solution.py:160
  844.1 12.8 %all_gather.73 = bf16[64,4096]{1,0:T(8,128)(2,1)S(1)} all-gather(bf16[64,1024]{1,0:T(8,128)(2,1)S(1)} %broadcast_select_fusion), channel_id=1, replica_groups=mesh['section'=2,'blk'=16,'mp'=4] {'mp'}, dimensions={1}, use_global_device_ids=true | all-gather | bytes 655360 | tf_op jit(solution)/shard_map/all_gather | solution.py:105
  857.9 6.1 fusion.137
  864.0 23.8 %all-gather.4 = bf16[1024,1,1,128]{3,0,2,1:T(8,128)(2,1)S(1)} all-gather(bf16[64,1,1,128]{3,0,2,1:T(8,128)(2,1)S(1)} %slice.281), channel_id=6, replica_groups=mesh['section'=2,'blk'=16,'mp'=4] {'blk'}, dimensions={0}, use_global_device_ids=true | all-gather | bytes 278528 | tf_op jit(solution)/shard_map/all_gather | solution.py:128
  888.0 23.3 %all_gather.75 = bf16[1024,1,128]{2,0,1:T(8,128)(2,1)S(1)} all-gather(bf16[64,1,128]{2,0,1:T(8,128)(2,1)S(1)} %pad_maximum_fusion.4), channel_id=1, replica_groups=mesh['section'=2,'blk'=16,'mp'=4] {'blk'}, dimensions={0}, use_global_device_ids=true | all-gather | bytes 278528 | tf_op jit(solution)/shard_map/all_gather | solution.py:127
  918.9 2.4 fusion.25
  922.1 18.1 %reduce-scatter.14.cloned.1.call-done = bf16[64,1024]{1,0:T(8,128)(2,1)} async-done(((bf16[64,4096]{1,0:T(8,128)(2,1)}), bf16[64,1024]{1,0:T(8,128)(2,1)}) %reduce-scatter.14.cloned.1.call-update) | async-done | bytes 131088 | tf_op jit(solution)/shard_map/reduce_scatter | solution.py:160
  (292 shorter events, 68.8 us)
Async XLA Ops:
  6.5 419.6 %all-gather.9.cloned.1.call-start = ((), (), s32[]{:S(2)}) async-start(), calls=%async_computation.5 | async-start | bytes 2228224 | tf_op jit(solution)/shard_map/all_gather | solution.py:74
  7.3 473.2 %all-gather.11.cloned.1.call-start = ((), (), s32[]{:S(2)}) async-start(), calls=%async_computation.6 | async-start | bytes 8912896 | tf_op jit(solution)/shard_map/all_gather | solution.py:73
  8.0 494.1 %all-gather.13.cloned.1.call-start = ((), (), s32[]{:S(2)}) async-start(), calls=%async_computation.7 | async-start | bytes 8912896 | tf_op jit(solution)/shard_map/all_gather | solution.py:75
  8.7 517.9 %reduce-scatter.6.cloned.1.call-start = ((), (), s32[]{:S(2)}) async-start(), calls=%async_computation.8 | async-start | bytes 655360 | tf_op jit(solution)/shard_map/reduce_scatter | solution.py:160
  21.4 385.4 %copy-start.25 = (s32[256]{0:T(256)S(1)}, s32[256]{0:T(256)}, u32[]{:S(2)}) copy-start(s32[256]{0:T(256)} %param.18) | copy-start | bytes 3076
  21.4 403.2 %slice-start.8 = ((s32[4096]{0:T(1024)}), s32[1024]{0:T(1024)S(1)}, s32[]{:S(2)}) async-start(s32[4096]{0:T(1024)} %param.19), calls=%async_computation.21 | async-start | bytes 8192 | tf_op jit(solution)/shard_map/slice | solution.py:149
  21.4 404.6 %copy-start.46 = (f32[64]{0:T(128)}, f32[64]{0:T(128)S(1)}, u32[]{:S(2)}) copy-start(f32[64]{0:T(128)S(1)} %get-tuple-element.74) | copy-start | bytes 772
  22.2 554.2 %copy-start.26 = (f32[64]{0:T(128)}, f32[64]{0:T(128)S(1)}, u32[]{:S(2)}) copy-start(f32[64]{0:T(128)S(1)} %multiply_exponential_fusion) | copy-start | bytes 772
  22.2 384.6 %copy-start.44 = (s32[64]{0:T(128)}, s32[64]{0:T(128)S(1)}, u32[]{:S(2)}) copy-start(s32[64]{0:T(128)S(1)} %iota_add_fusion.5) | copy-start | bytes 772
  22.3 384.5 %copy-start.29 = (s32[64]{0:T(128)}, s32[64]{0:T(128)S(1)}, u32[]{:S(2)}) copy-start(s32[64]{0:T(128)S(1)} %get-tuple-element.77) | copy-start | bytes 772
  22.3 403.8 %copy-start.40 = (f32[64]{0:T(128)}, f32[64]{0:T(128)S(1)}, u32[]{:S(2)}) copy-start(f32[64]{0:T(128)S(1)} %get-tuple-element.80) | copy-start | bytes 772
  22.3 403.8 %copy-start.42 = (f32[64]{0:T(128)}, f32[64]{0:T(128)S(1)}, u32[]{:S(2)}) copy-start(f32[64]{0:T(128)S(1)} %get-tuple-element.79) | copy-start | bytes 772
  22.3 384.5 %copy-start.32 = (s32[64]{0:T(128)}, s32[64]{0:T(128)S(1)}, u32[]{:S(2)}) copy-start(s32[64]{0:T(128)S(1)} %get-tuple-element.75) | copy-start | bytes 772
  22.3 384.5 %copy-start.34 = (s32[64]{0:T(128)}, s32[64]{0:T(128)S(1)}, u32[]{:S(2)}) copy-start(s32[64]{0:T(128)S(1)} %get-tuple-element.76) | copy-start | bytes 772
  22.3 403.7 %copy-start.36 = (f32[64]{0:T(128)}, f32[64]{0:T(128)S(1)}, u32[]{:S(2)}) copy-start(f32[64]{0:T(128)S(1)} %get-tuple-element.82) | copy-start | bytes 772
  22.4 403.7 %copy-start.38 = (f32[64]{0:T(128)}, f32[64]{0:T(128)S(1)}, u32[]{:S(2)}) copy-start(f32[64]{0:T(128)S(1)} %get-tuple-element.81) | copy-start | bytes 772
  406.7 24.1 %copy-start.4 = (f32[1,4096]{1,0:T(1,128)S(1)}, f32[1,4096]{1,0:T(1,128)}, u32[]{:S(2)}) copy-start(f32[1,4096]{1,0:T(1,128)} %param.20) | copy-start | bytes 49156
  502.2 24.5 %copy-start.12 = (bf16[64,1024]{1,0:T(8,128)(2,1)S(1)}, bf16[64,1024]{1,0:T(8,128)(2,1)}, u32[]{:S(2)}) copy-start(bf16[64,1024]{1,0:T(8,128)(2,1)} %copy-done.11) | copy-start | bytes 393220
  502.2 28.6 %copy-start.50 = (pred[64]{0:T(512)(128)(4,1)S(1)}, pred[64]{0:T(512)(128)(4,1)}, u32[]{:S(2)}) copy-start(pred[64]{0:T(512)(128)(4,1)} %get-tuple-element.7) | copy-start | bytes 196
  508.0 122.6 %reduce-scatter.8.cloned.1.call-start = ((), (), s32[]{:S(2)}) async-start(), calls=%async_computation.9 | async-start | bytes 655360 | tf_op jit(solution)/shard_map/reduce_scatter | solution.py:160
  527.7 2.4 collective-permute-start
  546.4 29.9 %copy-start.43 = (f32[64]{0:T(128)S(1)}, f32[64]{0:T(128)}, u32[]{:S(2)}) copy-start(f32[64]{0:T(128)} %copy-done.42) | copy-start | bytes 772
  546.5 56.9 %copy-start.21 = (f32[64,64]{1,0:T(8,128)S(1)}, f32[64,64]{1,0:T(8,128)}, u32[]{:S(2)}) copy-start(f32[64,64]{1,0:T(8,128)} %get-tuple-element.51) | copy-start | bytes 49156
  546.5 56.9 %copy-start.22 = (f32[64,64]{1,0:T(8,128)S(1)}, f32[64,64]{1,0:T(8,128)}, u32[]{:S(2)}) copy-start(f32[64,64]{1,0:T(8,128)} %get-tuple-element.52) | copy-start | bytes 49156
  546.5 57.1 %copy-start.14 = (pred[64,2048]{1,0:T(8,128)(4,1)S(1)}, pred[64,2048]{1,0:T(8,128)(4,1)}, u32[]{:S(2)}) copy-start(pred[64,2048]{1,0:T(8,128)(4,1)} %compare_and_fusion.1) | copy-start | bytes 393220
  609.4 21.3 %copy-start.8 = (bf16[64,1024]{1,0:T(8,128)(2,1)S(1)}, bf16[64,1024]{1,0:T(8,128)(2,1)}, u32[]{:S(2)}) copy-start(bf16[64,1024]{1,0:T(8,128)(2,1)} %copy-done.7) | copy-start | bytes 393220
  611.8 121.7 %reduce-scatter.10.cloned.1.call-start = ((), (), s32[]{:S(2)}) async-start(), calls=%async_computation.10 | async-start | bytes 655360 | tf_op jit(solution)/shard_map/reduce_scatter | solution.py:160
  631.6 2.3 collective-permute-start.1
  648.5 29.9 %copy-start.27 = (f32[64]{0:T(128)S(1)}, f32[64]{0:T(128)}, u32[]{:S(2)}) copy-start(f32[64]{0:T(128)} %copy-done.26) | copy-start | bytes 772
  648.5 29.9 %copy-start.41 = (f32[64]{0:T(128)S(1)}, f32[64]{0:T(128)}, u32[]{:S(2)}) copy-start(f32[64]{0:T(128)} %copy-done.40) | copy-start | bytes 772
  648.5 57.1 %copy-start.19 = (f32[64,64]{1,0:T(8,128)S(1)}, f32[64,64]{1,0:T(8,128)}, u32[]{:S(2)}) copy-start(f32[64,64]{1,0:T(8,128)} %get-tuple-element.53) | copy-start | bytes 49156
  648.5 57.1 %copy-start.20 = (f32[64,64]{1,0:T(8,128)S(1)}, f32[64,64]{1,0:T(8,128)}, u32[]{:S(2)}) copy-start(f32[64,64]{1,0:T(8,128)} %get-tuple-element.54) | copy-start | bytes 49156
  648.5 57.2 %copy-start.13 = (pred[64,3072]{1,0:T(8,128)(4,1)S(1)}, pred[64,3072]{1,0:T(8,128)(4,1)}, u32[]{:S(2)}) copy-start(pred[64,3072]{1,0:T(8,128)(4,1)} %compare_and_fusion) | copy-start | bytes 589828
  712.1 23.7 %copy-start.54 = (pred[64]{0:T(512)(128)(4,1)S(1)}, pred[64]{0:T(512)(128)(4,1)}, u32[]{:S(2)}) copy-start(pred[64]{0:T(512)(128)(4,1)} %get-tuple-element.9) | copy-start | bytes 196
  714.5 122.9 %reduce-scatter.12.cloned.1.call-start = ((), (), s32[]{:S(2)}) async-start(), calls=%async_computation.11 | async-start | bytes 655360 | tf_op jit(solution)/shard_map/reduce_scatter | solution.py:160
  734.5 2.5 collective-permute-start.2
  752.1 29.9 %copy-start.39 = (f32[64]{0:T(128)S(1)}, f32[64]{0:T(128)}, u32[]{:S(2)}) copy-start(f32[64]{0:T(128)} %copy-done.38) | copy-start | bytes 772
  752.1 56.9 %copy-start.17 = (f32[64,64]{1,0:T(8,128)S(1)}, f32[64,64]{1,0:T(8,128)}, u32[]{:S(2)}) copy-start(f32[64,64]{1,0:T(8,128)} %get-tuple-element.55) | copy-start | bytes 49156
  752.1 56.9 %copy-start.18 = (f32[64,64]{1,0:T(8,128)S(1)}, f32[64,64]{1,0:T(8,128)}, u32[]{:S(2)}) copy-start(f32[64,64]{1,0:T(8,128)} %get-tuple-element.56) | copy-start | bytes 49156
  752.1 57.0 %copy-start.3 = (pred[64,4096]{1,0:T(8,128)(4,1)S(1)}, pred[64,4096]{1,0:T(8,128)(4,1)}, u32[]{:S(2)}) copy-start(pred[64,4096]{1,0:T(8,128)(4,1)} %get-tuple-element.40) | copy-start | bytes 786436
  816.2 23.5 %copy-start.53 = (pred[64]{0:T(512)(128)(4,1)S(1)}, pred[64]{0:T(512)(128)(4,1)}, u32[]{:S(2)}) copy-start(pred[64]{0:T(512)(128)(4,1)} %get-tuple-element.6) | copy-start | bytes 196
  818.6 121.5 %reduce-scatter.14.cloned.1.call-start = ((), (), s32[]{:S(2)}) async-start(), calls=%async_computation.12 | async-start | bytes 655360 | tf_op jit(solution)/shard_map/reduce_scatter | solution.py:160
  838.5 4.9 collective-permute-start.3
  857.9 29.9 %copy-start.28 = (f32[64]{0:T(128)S(1)}, f32[64]{0:T(128)}, u32[]{:S(2)}) copy-start(f32[64]{0:T(128)} %copy-done.26) | copy-start | bytes 772
  857.9 29.8 %copy-start.37 = (f32[64]{0:T(128)S(1)}, f32[64]{0:T(128)}, u32[]{:S(2)}) copy-start(f32[64]{0:T(128)} %copy-done.36) | copy-start | bytes 772
  857.9 55.5 %copy-start.16 = (f32[64,64]{1,0:T(8,128)S(1)}, f32[64,64]{1,0:T(8,128)}, u32[]{:S(2)}) copy-start(f32[64,64]{1,0:T(8,128)} %get-tuple-element.42) | copy-start | bytes 49156
  918.9 21.3 %copy-start.10 = (bf16[64,1024]{1,0:T(8,128)(2,1)S(1)}, bf16[64,1024]{1,0:T(8,128)(2,1)}, u32[]{:S(2)}) copy-start(bf16[64,1024]{1,0:T(8,128)(2,1)} %copy-done.9) | copy-start | bytes 393220
  918.9 22.9 %copy-start.1 = (bf16[5120,80]{0,1:T(8,128)(2,1)S(1)}, bf16[5120,80]{0,1:T(8,128)(2,1)}, u32[]{:S(2)}) copy-start(bf16[5120,80]{0,1:T(8,128)(2,1)} %param.15) | copy-start | bytes 2457604
  (34 other events, 187.1 us)
Sparse Core Ops, SparseCore 0:
  9.5 47.7 all-gather.8
  59.5 74.0 all-gather.10
  135.7 81.8 all-gather.12
  508.1 18.4 reduce-scatter.5
  611.9 18.7 reduce-scatter.7
  714.6 18.8 reduce-scatter.9
  818.8 18.6 reduce-scatter.11
  921.4 18.7 reduce-scatter.13
where the time goes:
time: 957 us; the launch traced here: 949 us
  blocking collectives  685 us (72%)
  waiting for transfers between devices  87 us (9%)
  matrix products  81.5 us (9%)
  other arithmetic  37.5 us (4%)
  local copies, waits for them, and re-layouts  37.3 us (4%)
  between operations  15.1 us (2%)
    psum x1, blocking collectives, local(): merged_full = lax.psum(partial_merge, ('blk', 'mp')).astype(jnp.bfloat16)  383 us
    all_gather x5, blocking collectives, local(): lax.all_gather(new_values, 'blk', axis=0, tiled=True)  119 us
    all_gather x5, blocking collectives, local(): lax.all_gather(new_keys, 'blk', axis=0, tiled=True)  114 us
    reduce_scatter x5, waiting for transfers between devices, local(): lax.psum_scatter(term.astype(jnp.bfloat16), 'mp', scatter_dimension=1, ti...  84.4 us
    all_gather x5, blocking collectives, local(): features = lax.all_gather(incoming, 'mp', axis=1, tiled=True)  66.5 us
    dot_general x5, matrix products, local(): jnp.dot(normx, query_full, preferred_element_type=jnp.float32)  30.4 us
  transfers between devices with their start and end apart: 12, of which 6 were waited for; matrix products, arithmetic and copies ran while one was open for 7% of the time, Pallas kernels for 0%

commit v1 on v0

--- a/solution.py
+++ b/solution.py
@@ -66,7 +66,7 @@
         jnp.dot(normed, merge_first, preferred_element_type=jnp.float32), approximate=False
     ).astype(jnp.bfloat16)
     partial_merge = jnp.dot(inner, merge_second, preferred_element_type=jnp.float32)
-    merged_full = lax.psum(partial_merge, ("blk", "mp")).astype(jnp.bfloat16)
+    merged_full = lax.psum(lax.psum(partial_merge, "mp"), "blk").astype(jnp.bfloat16)
     merged_mine = lax.dynamic_slice_in_dim(merged_full, model_index * slice_width, slice_width, 1)
     visual_all = lax.all_gather(merged_mine, "section", axis=0, tiled=True)
     query_full, keyval_full, out_full = (

time: 957 us -> 740 us (0.77)
  blocking collectives: 685 us -> 410 us
  waiting for transfers between devices: 87 us -> 142 us
    psum x1, blocking collectives: 383 us -> 109 us  [local(): lax.psum(lax.psum(partial_merge, 'mp'), 'blk').astype(jnp.bfloat16)]
    psum x0 -> x1, waiting for transfers between devices: none -> 55.4 us  [local(): lax.psum(partial_merge, 'mp')]
  transfers between devices with their start and end apart: 12 -> 13, of which waited for: 6 -> 6; matrix products, arithmetic and copies ran while one was open for 7% -> 7% of each run, Pallas kernels for 0% -> 0%
where the time goes in v1:
time: 740 us; the launch traced here: 731 us
  blocking collectives  410 us (55%)
  waiting for transfers between devices  142 us (19%)
  matrix products  81.7 us (11%)
  other arithmetic  37.5 us (5%)
  local copies, waits for them, and re-layouts  37 us (5%)
  between operations  16.7 us (2%)
    all_gather x5, blocking collectives, local(): lax.all_gather(new_values, 'blk', axis=0, tiled=True)  119 us
    all_gather x5, blocking collectives, local(): lax.all_gather(new_keys, 'blk', axis=0, tiled=True)  114 us
    psum x1, blocking collectives, local(): lax.psum(lax.psum(partial_merge, 'mp'), 'blk').astype(jnp.bfloat16)  109 us
    reduce_scatter x5, waiting for transfers between devices, local(): lax.psum_scatter(term.astype(jnp.bfloat16), 'mp', scatter_dimension=1, ti...  85.1 us
    all_gather x5, blocking collectives, local(): features = lax.all_gather(incoming, 'mp', axis=1, tiled=True)  65.8 us
    psum x1, waiting for transfers between devices, local(): lax.psum(partial_merge, 'mp')  55.4 us
    dot_general x5, matrix products, local(): jnp.dot(normx, query_full, preferred_element_type=jnp.float32)  30.4 us
    dot_general x5, matrix products, local(): term = jnp.dot(attended, out_full, preferred_element_type=jnp.float32)  15.2 us
  transfers between devices with their start and end apart: 13, of which 6 were waited for; matrix products, arithmetic and copies ran while one was open for 7% of the time, Pallas kernels for 0%

profile of v1, /device:TPU:0, one launch (start us, length us, event | category | flops | bytes accessed | tf_op | source)
XLA Modules:
  0.0 731.1 jit_solution(2510910053995191447)
XLA Ops:
  7.4 2.9 reshape.1266
  12.9 1.9 copy.38
  14.9 5.4 fusion.210
  26.5 55.4 %all-reduce.3.cloned.1.call-done = f32[128,4096]{1,0:T(8,128)} async-done(((f32[128,4096]{1,0:T(8,128)}), f32[128,4096]{1,0:T(8,128)}) %all-reduce.3.cloned.1.call-update) | async-done | bytes 2097168 | tf_op jit(solution)/shard_map/psum | solution.py:69
  81.9 108.8 %all-reduce.4 = bf16[128,4096]{1,0:T(8,128)(2,1)S(1)} all-reduce(f32[128,4096]{1,0:T(8,128)} %all-reduce.3.cloned.1.call-done), channel_id=1, replica_groups=mesh['section'=2,'blk'=16,'mp'=4] {'blk'}, use_global_device_ids=true, to_apply=%region_4.5 | all-reduce | flops 524288 | bytes 3145728 | tf_op jit(solution)/shard_map/psum | solution.py:69
  190.8 2.2 all_gather.57
  194.2 12.8 %all_gather.58 = bf16[64,4096]{1,0:T(8,128)(2,1)S(1)} all-gather(bf16[64,1024]{1,0:T(8,128)(2,1)S(1)} %fusion.63), channel_id=1, replica_groups=mesh['section'=2,'blk'=16,'mp'=4] {'mp'}, dimensions={1}, use_global_device_ids=true | all-gather | bytes 655360 | tf_op jit(solution)/shard_map/all_gather | solution.py:105
  207.2 4.7 copy.37
  213.1 21.3 %all_gather.61 = bf16[1024,1,128]{2,0,1:T(8,128)(2,1)S(1)} all-gather(bf16[64,1,128]{2,0,1:T(8,128)(2,1)S(1)} %pad_maximum_fusion), channel_id=1, replica_groups=mesh['section'=2,'blk'=16,'mp'=4] {'blk'}, dimensions={0}, use_global_device_ids=true | all-gather | bytes 278528 | tf_op jit(solution)/shard_map/all_gather | solution.py:127
  234.3 24.3 %all-gather = bf16[1024,1,1,128]{3,0,2,1:T(8,128)(2,1)S(1)} all-gather(bf16[64,1,1,128]{3,0,2,1:T(8,128)(2,1)S(1)} %slice.285), channel_id=2, replica_groups=mesh['section'=2,'blk'=16,'mp'=4] {'blk'}, dimensions={0}, use_global_device_ids=true | all-gather | bytes 278528 | tf_op jit(solution)/shard_map/all_gather | solution.py:128
  262.4 11.4 %copy.31 = bf16[1024,4096]{1,0:T(8,128)(2,1)} copy(bf16[1024,4096]{0,1:T(8,128)(2,1)} %bitcast.333) | data formatting | bytes 16777216 | tf_op jit(solution)/shard_map/dot_general | solution.py:113
  273.8 6.1 fusion.125
  283.8 5.8 fusion.13
  292.8 15.5 %reduce-scatter.6.cloned.1.call-done = bf16[64,1024]{1,0:T(8,128)(2,1)} async-done(((bf16[64,4096]{1,0:T(8,128)(2,1)}), bf16[64,1024]{1,0:T(8,128)(2,1)}) %reduce-scatter.6.cloned.1.call-update) | async-done | bytes 131088 | tf_op jit(solution)/shard_map/reduce_scatter | solution.py:160
  313.6 13.5 %all_gather.64 = bf16[64,4096]{1,0:T(8,128)(2,1)S(1)} all-gather(bf16[64,1024]{1,0:T(8,128)(2,1)S(1)} %fusion.65), channel_id=1, replica_groups=mesh['section'=2,'blk'=16,'mp'=4] {'mp'}, dimensions={1}, use_global_device_ids=true | all-gather | bytes 655360 | tf_op jit(solution)/shard_map/all_gather | solution.py:105
  328.2 6.1 fusion.128
  334.3 23.7 %all-gather.1 = bf16[1024,1,1,128]{3,0,2,1:T(8,128)(2,1)S(1)} all-gather(bf16[64,1,1,128]{3,0,2,1:T(8,128)(2,1)S(1)} %slice.284), channel_id=3, replica_groups=mesh['section'=2,'blk'=16,'mp'=4] {'blk'}, dimensions={0}, use_global_device_ids=true | all-gather | bytes 278528 | tf_op jit(solution)/shard_map/all_gather | solution.py:128
  358.3 23.3 %all_gather.66 = bf16[1024,1,128]{2,0,1:T(8,128)(2,1)S(1)} all-gather(bf16[64,1,128]{2,0,1:T(8,128)(2,1)S(1)} %pad_maximum_fusion.1), channel_id=1, replica_groups=mesh['section'=2,'blk'=16,'mp'=4] {'blk'}, dimensions={0}, use_global_device_ids=true | all-gather | bytes 278528 | tf_op jit(solution)/shard_map/all_gather | solution.py:127
  381.5 1.7 fusion.142
  385.2 2.0 fusion.312
  387.8 2.2 fusion.69
  391.0 2.4 fusion.16
  397.1 15.1 %reduce-scatter.8.cloned.1.call-done = bf16[64,1024]{1,0:T(8,128)(2,1)} async-done(((bf16[64,4096]{1,0:T(8,128)(2,1)}), bf16[64,1024]{1,0:T(8,128)(2,1)}) %reduce-scatter.8.cloned.1.call-update) | async-done | bytes 131088 | tf_op jit(solution)/shard_map/reduce_scatter | solution.py:160
  415.7 13.4 %all_gather.67 = bf16[64,4096]{1,0:T(8,128)(2,1)S(1)} all-gather(bf16[64,1024]{1,0:T(8,128)(2,1)S(1)} %broadcast_select_fusion.2), channel_id=1, replica_groups=mesh['section'=2,'blk'=16,'mp'=4] {'mp'}, dimensions={1}, use_global_device_ids=true | all-gather | bytes 655360 | tf_op jit(solution)/shard_map/all_gather | solution.py:105
  430.2 6.1 fusion.131
  436.3 23.7 %all-gather.2 = bf16[1024,1,1,128]{3,0,2,1:T(8,128)(2,1)S(1)} all-gather(bf16[64,1,1,128]{3,0,2,1:T(8,128)(2,1)S(1)} %slice.283), channel_id=4, replica_groups=mesh['section'=2,'blk'=16,'mp'=4] {'blk'}, dimensions={0}, use_global_device_ids=true | all-gather | bytes 278528 | tf_op jit(solution)/shard_map/all_gather | solution.py:128
  460.3 23.4 %all_gather.69 = bf16[1024,1,128]{2,0,1:T(8,128)(2,1)S(1)} all-gather(bf16[64,1,128]{2,0,1:T(8,128)(2,1)S(1)} %pad_maximum_fusion.2), channel_id=1, replica_groups=mesh['section'=2,'blk'=16,'mp'=4] {'blk'}, dimensions={0}, use_global_device_ids=true | all-gather | bytes 278528 | tf_op jit(solution)/shard_map/all_gather | solution.py:127
  485.5 1.7 select_dynamic-update-slice_fusion.1
  487.4 2.4 fusion.313
  490.8 2.5 fusion.79
  493.8 2.4 fusion.19
  497.4 17.7 %reduce-scatter.10.cloned.1.call-done = bf16[64,1024]{1,0:T(8,128)(2,1)} async-done(((bf16[64,4096]{1,0:T(8,128)(2,1)}), bf16[64,1024]{1,0:T(8,128)(2,1)}) %reduce-scatter.10.cloned.1.call-update) | async-done | bytes 131088 | tf_op jit(solution)/shard_map/reduce_scatter | solution.py:160
  519.3 13.4 %all_gather.70 = bf16[64,4096]{1,0:T(8,128)(2,1)S(1)} all-gather(bf16[64,1024]{1,0:T(8,128)(2,1)S(1)} %broadcast_select_fusion.1), channel_id=1, replica_groups=mesh['section'=2,'blk'=16,'mp'=4] {'mp'}, dimensions={1}, use_global_device_ids=true | all-gather | bytes 655360 | tf_op jit(solution)/shard_map/all_gather | solution.py:105
  533.7 6.1 fusion.134
  539.8 23.8 %all-gather.3 = bf16[1024,1,1,128]{3,0,2,1:T(8,128)(2,1)S(1)} all-gather(bf16[64,1,1,128]{3,0,2,1:T(8,128)(2,1)S(1)} %slice.282), channel_id=5, replica_groups=mesh['section'=2,'blk'=16,'mp'=4] {'blk'}, dimensions={0}, use_global_device_ids=true | all-gather | bytes 278528 | tf_op jit(solution)/shard_map/all_gather | solution.py:128
  563.9 23.2 %all_gather.72 = bf16[1024,1,128]{2,0,1:T(8,128)(2,1)S(1)} all-gather(bf16[64,1,128]{2,0,1:T(8,128)(2,1)S(1)} %pad_maximum_fusion.3), channel_id=1, replica_groups=mesh['section'=2,'blk'=16,'mp'=4] {'blk'}, dimensions={0}, use_global_device_ids=true | all-gather | bytes 278528 | tf_op jit(solution)/shard_map/all_gather | solution.py:127
  587.1 1.7 fusion.140
  588.8 1.7 select_dynamic-update-slice_fusion
  590.7 2.9 fusion.314
  594.9 2.8 fusion.76
  597.8 2.4 fusion.22
  600.3 18.8 %reduce-scatter.12.cloned.1.call-done = bf16[64,1024]{1,0:T(8,128)(2,1)} async-done(((bf16[64,4096]{1,0:T(8,128)(2,1)}), bf16[64,1024]{1,0:T(8,128)(2,1)}) %reduce-scatter.12.cloned.1.call-update) | async-done | bytes 131088 | tf_op jit(solution)/shard_map/reduce_scatter | solution.py:160
  625.7 12.8 %all_gather.73 = bf16[64,4096]{1,0:T(8,128)(2,1)S(1)} all-gather(bf16[64,1024]{1,0:T(8,128)(2,1)S(1)} %broadcast_select_fusion), channel_id=1, replica_groups=mesh['section'=2,'blk'=16,'mp'=4] {'mp'}, dimensions={1}, use_global_device_ids=true | all-gather | bytes 655360 | tf_op jit(solution)/shard_map/all_gather | solution.py:105
  639.5 6.1 fusion.137
  645.6 23.7 %all-gather.4 = bf16[1024,1,1,128]{3,0,2,1:T(8,128)(2,1)S(1)} all-gather(bf16[64,1,1,128]{3,0,2,1:T(8,128)(2,1)S(1)} %slice.281), channel_id=6, replica_groups=mesh['section'=2,'blk'=16,'mp'=4] {'blk'}, dimensions={0}, use_global_device_ids=true | all-gather | bytes 278528 | tf_op jit(solution)/shard_map/all_gather | solution.py:128
  669.6 23.3 %all_gather.75 = bf16[1024,1,128]{2,0,1:T(8,128)(2,1)S(1)} all-gather(bf16[64,1,128]{2,0,1:T(8,128)(2,1)S(1)} %pad_maximum_fusion.4), channel_id=1, replica_groups=mesh['section'=2,'blk'=16,'mp'=4] {'blk'}, dimensions={0}, use_global_device_ids=true | all-gather | bytes 278528 | tf_op jit(solution)/shard_map/all_gather | solution.py:127
  700.5 2.4 fusion.25
  703.7 18.1 %reduce-scatter.14.cloned.1.call-done = bf16[64,1024]{1,0:T(8,128)(2,1)} async-done(((bf16[64,4096]{1,0:T(8,128)(2,1)}), bf16[64,1024]{1,0:T(8,128)(2,1)}) %reduce-scatter.14.cloned.1.call-update) | async-done | bytes 131088 | tf_op jit(solution)/shard_map/reduce_scatter | solution.py:160
  (297 shorter events, 69.7 us)
Async XLA Ops:
  7.4 74.5 %all-reduce.3.cloned.1.call-start = ((), (), s32[]{:S(2)}) async-start(), calls=%async_computation.5 | async-start | bytes 4194304 | tf_op jit(solution)/shard_map/psum | solution.py:69
  20.2 172.7 %copy-start.26 = (s32[256]{0:T(256)S(1)}, s32[256]{0:T(256)}, u32[]{:S(2)}) copy-start(s32[256]{0:T(256)} %param.18) | copy-start | bytes 3076
  20.3 186.9 %all-gather.9.cloned.1.call-start = ((), (), s32[]{:S(2)}) async-start(), calls=%async_computation.6 | async-start | bytes 2228224 | tf_op jit(solution)/shard_map/all_gather | solution.py:74
  20.9 241.5 %all-gather.11.cloned.1.call-start = ((), (), s32[]{:S(2)}) async-start(), calls=%async_computation.7 | async-start | bytes 8912896 | tf_op jit(solution)/shard_map/all_gather | solution.py:73
  21.4 262.3 %all-gather.13.cloned.1.call-start = ((), (), s32[]{:S(2)}) async-start(), calls=%async_computation.8 | async-start | bytes 8912896 | tf_op jit(solution)/shard_map/all_gather | solution.py:75
  22.0 286.3 %reduce-scatter.6.cloned.1.call-start = ((), (), s32[]{:S(2)}) async-start(), calls=%async_computation.9 | async-start | bytes 655360 | tf_op jit(solution)/shard_map/reduce_scatter | solution.py:160
  22.1 168.5 %copy-start.47 = (f32[64]{0:T(128)}, f32[64]{0:T(128)S(1)}, u32[]{:S(2)}) copy-start(f32[64]{0:T(128)S(1)} %get-tuple-element.74) | copy-start | bytes 772
  22.9 335.1 %copy-start.27 = (f32[64]{0:T(128)}, f32[64]{0:T(128)S(1)}, u32[]{:S(2)}) copy-start(f32[64]{0:T(128)S(1)} %multiply_exponential_fusion) | copy-start | bytes 772
  23.0 167.7 %copy-start.45 = (s32[64]{0:T(128)}, s32[64]{0:T(128)S(1)}, u32[]{:S(2)}) copy-start(s32[64]{0:T(128)S(1)} %iota_add_fusion.5) | copy-start | bytes 772
  23.0 189.0 %copy-start.30 = (s32[64]{0:T(128)}, s32[64]{0:T(128)S(1)}, u32[]{:S(2)}) copy-start(s32[64]{0:T(128)S(1)} %get-tuple-element.77) | copy-start | bytes 772
  23.0 167.7 %copy-start.41 = (f32[64]{0:T(128)}, f32[64]{0:T(128)S(1)}, u32[]{:S(2)}) copy-start(f32[64]{0:T(128)S(1)} %get-tuple-element.80) | copy-start | bytes 772
  23.0 167.7 %copy-start.43 = (f32[64]{0:T(128)}, f32[64]{0:T(128)S(1)}, u32[]{:S(2)}) copy-start(f32[64]{0:T(128)S(1)} %get-tuple-element.79) | copy-start | bytes 772
  23.0 167.7 %copy-start.33 = (s32[64]{0:T(128)}, s32[64]{0:T(128)S(1)}, u32[]{:S(2)}) copy-start(s32[64]{0:T(128)S(1)} %get-tuple-element.75) | copy-start | bytes 772
  23.0 167.7 %copy-start.35 = (s32[64]{0:T(128)}, s32[64]{0:T(128)S(1)}, u32[]{:S(2)}) copy-start(s32[64]{0:T(128)S(1)} %get-tuple-element.76) | copy-start | bytes 772
  23.1 167.7 %copy-start.37 = (f32[64]{0:T(128)}, f32[64]{0:T(128)S(1)}, u32[]{:S(2)}) copy-start(f32[64]{0:T(128)S(1)} %get-tuple-element.82) | copy-start | bytes 772
  23.1 167.7 %copy-start.39 = (f32[64]{0:T(128)}, f32[64]{0:T(128)S(1)}, u32[]{:S(2)}) copy-start(f32[64]{0:T(128)S(1)} %get-tuple-element.81) | copy-start | bytes 772
  194.1 40.2 %copy-start.11 = (bf16[64,1024]{1,0:T(8,128)(2,1)}, bf16[64,1024]{1,0:T(8,128)(2,1)S(1)}, u32[]{:S(2)}) copy-start(bf16[64,1024]{1,0:T(8,128)(2,1)S(1)} %fusion.63) | copy-start | bytes 393220
  283.8 24.6 %copy-start.12 = (bf16[64,1024]{1,0:T(8,128)(2,1)S(1)}, bf16[64,1024]{1,0:T(8,128)(2,1)}, u32[]{:S(2)}) copy-start(bf16[64,1024]{1,0:T(8,128)(2,1)} %copy-done.11) | copy-start | bytes 393220
  283.8 28.6 %copy-start.51 = (pred[64]{0:T(512)(128)(4,1)S(1)}, pred[64]{0:T(512)(128)(4,1)}, u32[]{:S(2)}) copy-start(pred[64]{0:T(512)(128)(4,1)} %get-tuple-element.7) | copy-start | bytes 196
  289.6 122.6 %reduce-scatter.8.cloned.1.call-start = ((), (), s32[]{:S(2)}) async-start(), calls=%async_computation.10 | async-start | bytes 655360 | tf_op jit(solution)/shard_map/reduce_scatter | solution.py:160
  309.3 2.4 collective-permute-start
  328.1 29.9 %copy-start.44 = (f32[64]{0:T(128)S(1)}, f32[64]{0:T(128)}, u32[]{:S(2)}) copy-start(f32[64]{0:T(128)} %copy-done.43) | copy-start | bytes 772
  328.1 56.9 %copy-start.21 = (f32[64,64]{1,0:T(8,128)S(1)}, f32[64,64]{1,0:T(8,128)}, u32[]{:S(2)}) copy-start(f32[64,64]{1,0:T(8,128)} %get-tuple-element.51) | copy-start | bytes 49156
  328.1 56.9 %copy-start.22 = (f32[64,64]{1,0:T(8,128)S(1)}, f32[64,64]{1,0:T(8,128)}, u32[]{:S(2)}) copy-start(f32[64,64]{1,0:T(8,128)} %get-tuple-element.52) | copy-start | bytes 49156
  328.1 57.0 %copy-start.14 = (pred[64,2048]{1,0:T(8,128)(4,1)S(1)}, pred[64,2048]{1,0:T(8,128)(4,1)}, u32[]{:S(2)}) copy-start(pred[64,2048]{1,0:T(8,128)(4,1)} %compare_and_fusion.1) | copy-start | bytes 393220
  390.9 21.3 %copy-start.8 = (bf16[64,1024]{1,0:T(8,128)(2,1)S(1)}, bf16[64,1024]{1,0:T(8,128)(2,1)}, u32[]{:S(2)}) copy-start(bf16[64,1024]{1,0:T(8,128)(2,1)} %copy-done.7) | copy-start | bytes 393220
  391.0 23.6 %copy-start.56 = (pred[64]{0:T(512)(128)(4,1)S(1)}, pred[64]{0:T(512)(128)(4,1)}, u32[]{:S(2)}) copy-start(pred[64]{0:T(512)(128)(4,1)} %get-tuple-element.8) | copy-start | bytes 196
  393.4 121.7 %reduce-scatter.10.cloned.1.call-start = ((), (), s32[]{:S(2)}) async-start(), calls=%async_computation.11 | async-start | bytes 655360 | tf_op jit(solution)/shard_map/reduce_scatter | solution.py:160
  413.2 2.5 collective-permute-start.1
  430.2 29.9 %copy-start.28 = (f32[64]{0:T(128)S(1)}, f32[64]{0:T(128)}, u32[]{:S(2)}) copy-start(f32[64]{0:T(128)} %copy-done.27) | copy-start | bytes 772
  430.2 29.9 %copy-start.42 = (f32[64]{0:T(128)S(1)}, f32[64]{0:T(128)}, u32[]{:S(2)}) copy-start(f32[64]{0:T(128)} %copy-done.41) | copy-start | bytes 772
  430.2 57.0 %copy-start.19 = (f32[64,64]{1,0:T(8,128)S(1)}, f32[64,64]{1,0:T(8,128)}, u32[]{:S(2)}) copy-start(f32[64,64]{1,0:T(8,128)} %get-tuple-element.53) | copy-start | bytes 49156
  430.2 57.0 %copy-start.20 = (f32[64,64]{1,0:T(8,128)S(1)}, f32[64,64]{1,0:T(8,128)}, u32[]{:S(2)}) copy-start(f32[64,64]{1,0:T(8,128)} %get-tuple-element.54) | copy-start | bytes 49156
  430.2 57.2 %copy-start.13 = (pred[64,3072]{1,0:T(8,128)(4,1)S(1)}, pred[64,3072]{1,0:T(8,128)(4,1)}, u32[]{:S(2)}) copy-start(pred[64,3072]{1,0:T(8,128)(4,1)} %compare_and_fusion) | copy-start | bytes 589828
  493.8 23.7 %copy-start.55 = (pred[64]{0:T(512)(128)(4,1)S(1)}, pred[64]{0:T(512)(128)(4,1)}, u32[]{:S(2)}) copy-start(pred[64]{0:T(512)(128)(4,1)} %get-tuple-element.9) | copy-start | bytes 196
  496.2 122.9 %reduce-scatter.12.cloned.1.call-start = ((), (), s32[]{:S(2)}) async-start(), calls=%async_computation.12 | async-start | bytes 655360 | tf_op jit(solution)/shard_map/reduce_scatter | solution.py:160
  516.1 2.5 collective-permute-start.2
  533.7 29.9 %copy-start.40 = (f32[64]{0:T(128)S(1)}, f32[64]{0:T(128)}, u32[]{:S(2)}) copy-start(f32[64]{0:T(128)} %copy-done.39) | copy-start | bytes 772
  533.7 56.9 %copy-start.17 = (f32[64,64]{1,0:T(8,128)S(1)}, f32[64,64]{1,0:T(8,128)}, u32[]{:S(2)}) copy-start(f32[64,64]{1,0:T(8,128)} %get-tuple-element.55) | copy-start | bytes 49156
  533.7 56.9 %copy-start.18 = (f32[64,64]{1,0:T(8,128)S(1)}, f32[64,64]{1,0:T(8,128)}, u32[]{:S(2)}) copy-start(f32[64,64]{1,0:T(8,128)} %get-tuple-element.56) | copy-start | bytes 49156
  533.7 57.0 %copy-start.3 = (pred[64,4096]{1,0:T(8,128)(4,1)S(1)}, pred[64,4096]{1,0:T(8,128)(4,1)}, u32[]{:S(2)}) copy-start(pred[64,4096]{1,0:T(8,128)(4,1)} %get-tuple-element.40) | copy-start | bytes 786436
  597.8 23.6 %copy-start.54 = (pred[64]{0:T(512)(128)(4,1)S(1)}, pred[64]{0:T(512)(128)(4,1)}, u32[]{:S(2)}) copy-start(pred[64]{0:T(512)(128)(4,1)} %get-tuple-element.6) | copy-start | bytes 196
  600.2 121.5 %reduce-scatter.14.cloned.1.call-start = ((), (), s32[]{:S(2)}) async-start(), calls=%async_computation.13 | async-start | bytes 655360 | tf_op jit(solution)/shard_map/reduce_scatter | solution.py:160
  620.1 4.9 collective-permute-start.3
  639.5 29.8 %copy-start.29 = (f32[64]{0:T(128)S(1)}, f32[64]{0:T(128)}, u32[]{:S(2)}) copy-start(f32[64]{0:T(128)} %copy-done.27) | copy-start | bytes 772
  639.5 29.8 %copy-start.38 = (f32[64]{0:T(128)S(1)}, f32[64]{0:T(128)}, u32[]{:S(2)}) copy-start(f32[64]{0:T(128)} %copy-done.37) | copy-start | bytes 772
  639.5 55.5 %copy-start.16 = (f32[64,64]{1,0:T(8,128)S(1)}, f32[64,64]{1,0:T(8,128)}, u32[]{:S(2)}) copy-start(f32[64,64]{1,0:T(8,128)} %get-tuple-element.42) | copy-start | bytes 49156
  700.5 22.9 %copy-start.1 = (bf16[5120,80]{0,1:T(8,128)(2,1)S(1)}, bf16[5120,80]{0,1:T(8,128)(2,1)}, u32[]{:S(2)}) copy-start(bf16[5120,80]{0,1:T(8,128)(2,1)} %param.15) | copy-start | bytes 2457604
  (36 other events, 233.7 us)
Sparse Core Ops, SparseCore 0:
  20.4 61.4 all-reduce.2
  289.7 18.5 reduce-scatter.5
  393.5 18.7 reduce-scatter.7
  496.3 18.7 reduce-scatter.9
  600.3 18.6 reduce-scatter.11
  703.0 18.6 reduce-scatter.13
Sparse Core Ops, SparseCore 1:
  23.1 47.4 all-gather.8
  72.8 99.5 all-gather.10
  174.6 79.8 all-gather.12
